TPU v7x, 32 devices: a whole 2x2x4 slice. The times are simulated.
32 devices in a mesh: pages: 16 (over z, x, core), tok: 2 (over y).
Axes of the slice: x: 2, y: 2, z: 4, core: 2. Of those that a mesh axis runs over, the one named last changes fastest.
Arguments:
- queries: bfloat16 [32, 32, 128], P('pages'), may hold values from -50 to 50
- pages: bfloat16 [16, 1024, 128], P('pages', 'tok'), may hold values from -10 to 10
- pad_counts: int32 [16], P('pages'), may hold values from 0 to 511
- labels: int32 [32, 16], P(None, 'pages'), may hold values 0 or 1
Outputs:
- query_grad: float32 [32, 32, 128], P('pages')
- page_grad: float32 [16, 1024, 128], P('pages', 'tok')
- page_loss: float32 [16], P('pages')
All inputs are finite; a program needn't handle non-finite values. No bound on the sum of `labels` on one device may be relied on, other than what follows from the above.
Results may differ from a plain program's by a relative error of at most 0.0025.
Values may be sent and summed in bfloat16 or wider, within the bound.
No kernel may reach another device: no remote copies, remote signals or barrier semaphores. Data moves between devices by JAX's collectives and lax.ppermute only.
A program may use at most 64 MiB of HBM per device.

v0:
```python
import math
import jax
import jax.numpy as jnp
from jax import lax
from jax.sharding import PartitionSpec as P

LP = 1024
MASKED = -1000000000.0
LOGIT_SPAN = 8.0
CENTRE_SHIFT = 0.5
FILL_SHARE = 0.75


def combined_all(value, axis, combine):
    everything = lax.all_gather(value, axis)
    first = everything[0]

    def lap(k, so_far):
        return combine(so_far, everything[k])

    return lax.fori_loop(1, lax.axis_size(axis), lap, first)


def combine_smooth(former, latter):
    highest = jnp.maximum(former, latter)
    return highest + jnp.log(jnp.exp(former - highest) + jnp.exp(latter - highest))


def on_device(queries, pages, pad_counts, labels):
    query_count, query_len, feature_width = queries.shape
    local_pages, local_tokens, _ = pages.shape
    score_scale = feature_width ** (-0.5)
    token_offset = lax.axis_index("tok") * local_tokens
    positions = token_offset + jnp.arange(local_tokens, dtype=jnp.int32)
    usable = positions[None, :] < (LP - pad_counts)[:, None]
    gathered = lax.all_gather(queries, "pages", axis=0, tiled=True)
    query_total = gathered.shape[0]
    row_count = query_total * query_len
    query_rows = gathered.reshape(row_count, feature_width)
    block_rows = math.gcd(row_count, 512)
    block_count = row_count // block_rows

    def scores_for(query_block, page_no):
        raw = (
            lax.dot_general(
                query_block,
                pages[page_no],
                (((1,), (1,)), ((), ())),
                preferred_element_type=jnp.float32,
            )
            * score_scale
        )
        return jnp.where(usable[page_no][None, :], raw, MASKED)

    def forward_block(block_index, running):
        offset = block_index * block_rows
        query_block = lax.dynamic_slice_in_dim(query_rows, offset, block_rows, 0)
        scores = scores_for(query_block, 0)
        highest = jnp.max(scores, axis=1)
        columns = [highest + jnp.log(jnp.sum(jnp.exp(scores - highest[:, None]), axis=1))]
        partial_value = jnp.stack(columns, axis=1)
        return lax.dynamic_update_slice_in_dim(running, partial_value, offset, 0)

    buffered = lax.fori_loop(
        0, block_count, forward_block, jnp.zeros((row_count, local_pages), jnp.float32)
    )
    smooth = combined_all(buffered, "tok", combine_smooth)
    similarity = smooth.reshape(query_total, query_len, local_pages).sum(axis=1)
    label_sign = 2.0 * labels.astype(jnp.float32) - 1.0
    logit_gain = LOGIT_SPAN / query_len
    centre = query_len * (CENTRE_SHIFT + math.log(FILL_SHARE * LP))
    logits = logit_gain * (similarity - centre)
    page_loss = jnp.sum(jax.nn.softplus(-label_sign * logits), axis=0)
    slope = logit_gain * (-label_sign * jax.nn.sigmoid(-label_sign * logits))
    row_slope = jnp.repeat(slope, query_len, axis=0)

    def backward_block(block_index, running):
        query_terms, page_terms = running
        offset = block_index * block_rows
        query_block = lax.dynamic_slice_in_dim(query_rows, offset, block_rows, 0)
        smooth_block = lax.dynamic_slice_in_dim(smooth, offset, block_rows, 0)
        slope_block = lax.dynamic_slice_in_dim(row_slope, offset, block_rows, 0)
        scores = scores_for(query_block, 0)
        weights = jnp.where(usable[0][None, :], jnp.exp(scores - smooth_block[:, 0][:, None]), 0.0)
        scaled = (weights * slope_block[:, 0][:, None]).astype(jnp.bfloat16)
        summed = jnp.dot(scaled, pages[0], preferred_element_type=jnp.float32)
        gradients = [
            lax.dot_general(
                scaled, query_block, (((0,), (0,)), ((), ())), preferred_element_type=jnp.float32
            )
        ]
        page_terms = page_terms + jnp.stack(gradients, axis=0)
        query_terms = lax.dynamic_update_slice_in_dim(query_terms, summed * score_scale, offset, 0)
        return (query_terms, page_terms)

    start_terms = (
        jnp.zeros((row_count, feature_width), jnp.float32),
        jnp.zeros((local_pages, local_tokens, feature_width), jnp.float32),
    )
    query_terms, page_terms = lax.fori_loop(0, block_count, backward_block, start_terms)
    page_grad = page_terms * score_scale
    owned = lax.psum_scatter(query_terms, "pages", scatter_dimension=0, tiled=True)
    owned = lax.psum(owned, "tok")
    query_grad = owned.reshape(query_count, query_len, feature_width)
    return (query_grad, page_grad, page_loss)


def solution(mesh):
    return jax.shard_map(
        on_device,
        mesh=mesh,
        in_specs=(P("pages", None, None), P("pages", "tok", None), P("pages"), P(None, "pages")),
        out_specs=(P("pages", None, None), P("pages", "tok", None), P("pages")),
        check_vma=False,
    )
```

profile of v0, /device:TPU:0, one launch (start us, length us, event | category | flops | bytes accessed | tf_op | source)
XLA Modules:
  0.0 112.6 jit_solution(9280587860546555923)
XLA Ops:
  7.2 0.0 reduce-scatter.2.cloned.1.call-start
  7.9 0.0 copy-start
  7.9 24.2 %all_gather.9 = bf16[32,32,128]{2,1,0:T(8,128)(2,1)S(1)} all-gather(bf16[2,32,128]{2,1,0:T(8,128)(2,1)} %param.8), channel_id=1, replica_groups=mesh['pages'=16,'tok'=2] {'pages'}, dimensions={0}, use_global_device_ids=true | all-gather | bytes 278528 | tf_op jit(solution)/shard_map/all_gather | solution.py:36
  32.1 0.0 copy-done
  32.1 1.2 %while.35 = (s32[]{:T(128)}, f32[1024,1]{0,1:T(1,128)S(1)}, bf16[1024,128]{1,0:T(8,128)(2,1)S(1)}, bf16[1,512,128]{2,1,0:T(8,128)(2,1)S(1)}, s32[]{:T(128)}, /*i...) while((s32[]{:T(128)}, f32[1024,1]{0,1:T(1,128)S(1)}, ...), condition=%wide.region_3.4_spmd.clone, body=%wide.region_0.3_spmd.clone.sunk | while | flops 68420104 | bytes 2376867 | solution.py:64
  32.1 0.3 fusion.38
  32.4 0.2 exponential_reduce_fusion.2
  32.7 0.3 fusion.38
  33.0 0.2 exponential_reduce_fusion.2
  33.2 4.4 %all-gather = f32[2048,1]{0,1:T(1,128)S(1)} all-gather(f32[1024,1]{0,1:T(1,128)S(1)} %get-tuple-element.249), channel_id=2, replica_groups=mesh['pages'=16,'tok'=2] {'tok'}, dimensions={0}, use_global_device_ids=true | all-gather | bytes 12288 | tf_op jit(solution)/shard_map/all_gather | solution.py:15
  37.6 0.1 squeeze.28
  37.7 0.1 squeeze.29
  37.8 0.0 copy-start.2
  37.8 0.1 add_reduce_fusion
  37.9 0.5 copy-done.2
  38.4 0.6 fusion.24
  39.1 0.1 broadcast_in_dim.84
  39.2 0.1 broadcast_in_dim.85
  39.3 2.4 %while.36 = (s32[]{:T(128)}, f32[1024,128]{1,0:T(8,128)S(1)}, f32[1,512,128]{2,1,0:T(8,128)S(1)}, bf16[1024,128]{1,0:T(8,128)(2,1)S(1)}, bf16[1,512,128]{2,1,0:T...) while((s32[]{:T(128)}, f32[1024,128]{1,0:T(8,128)S(1)}, ...), condition=%wide.region_6.7_spmd.clone, body=%wide.region_5.6_spmd.clone.sunk | while | flops 203097088 | bytes 2897109 | solution.py:100
  39.4 0.4 fusion.45
  39.8 0.4 fusion.47
  40.2 0.3 fusion.46
  40.5 0.4 fusion.45
  41.0 0.4 fusion.47
  41.4 0.3 fusion.46
  41.7 0.0 copy-start.1
  41.7 0.8 copy-done.1
  42.5 0.0 reduce-scatter.2.cloned.1.call-update
  42.5 0.7 broadcast_multiply_fusion
  43.2 52.9 %reduce-scatter.2.cloned.1.call-done = f32[64,128]{1,0:T(8,128)} async-done(((f32[1024,128]{1,0:T(8,128)}), f32[64,128]{1,0:T(8,128)}) %reduce-scatter.2.cloned.1.call-update) | async-done | bytes 32784 | tf_op jit(solution)/shard_map/reduce_scatter | solution.py:102
  96.2 9.6 %psum.7 = f32[2,32,128]{2,1,0:T(8,128)} all-reduce(f32[2,32,128]{2,1,0:T(8,128)} %bitcast.50), channel_id=1, replica_groups=mesh['pages'=16,'tok'=2] {'tok'}, use_global_device_ids=true, to_apply=%region_8.9 | all-reduce | flops 8192 | bytes 65536 | tf_op jit(solution)/shard_map/psum | solution.py:103
  (15 shorter events, 0.3 us)
Async XLA Ops:
  7.2 89.0 %reduce-scatter.2.cloned.1.call-start = ((), (), s32[]{:S(2)}) async-start(), calls=%async_computation.1 | async-start | bytes 557056 | tf_op jit(solution)/shard_map/reduce_scatter | solution.py:102
  7.9 24.2 %copy-start = (bf16[1,512,128]{2,1,0:T(8,128)(2,1)S(1)}, bf16[1,512,128]{2,1,0:T(8,128)(2,1)}, u32[]{:S(2)}) copy-start(bf16[1,512,128]{2,1,0:T(8,128)(2,1)} %param.9) | copy-start | bytes 393220
  37.8 0.7 copy-start.2
  41.7 0.8 copy-start.1
Sparse Core Ops, SparseCore 0:
  42.6 53.4 reduce-scatter.1
where the time goes:
time: 113 us
  waiting for transfers between devices  52.9 us (47%)
  blocking collectives  38.1 us (34%)
  between operations  14.7 us (13%)
  matrix products  2.87 us (3%)
  other arithmetic  2.05 us (2%)
  local copies, waits for them, and re-layouts  1.7 us (2%)
    reduce_scatter x1, waiting for transfers between devices, on_device(): lax.psum_scatter(query_terms, 'pages', scatter_dimension=0, tiled=True)  52.9 us
    all_gather x1, blocking collectives, on_device(): gathered = lax.all_gather(queries, 'pages', axis=0, tiled=True)  24.2 us
    psum x1, blocking collectives, on_device(): owned = lax.psum(owned, 'tok')  9.55 us
    all_gather x1, blocking collectives, combined_all(): everything = lax.all_gather(value, axis)  4.36 us
  transfers between devices with their start and end apart: 1, of which 1 were waited for; matrix products, arithmetic and copies ran while one was open for 1% of the time, Pallas kernels for 0%

commit v1 on v0

--- a/solution.py
+++ b/solution.py
@@ -9,6 +9,19 @@
 LOGIT_SPAN = 8.0
 CENTRE_SHIFT = 0.5
 FILL_SHARE = 0.75
+
+
+def ring_gather(x, axis, dim):
+    ways = lax.axis_size(axis)
+    up = [(d, (d + 1) % ways) for d in range(ways)]
+    down = [(d, (d - 1) % ways) for d in range(ways)]
+    earlier, later = ([x], [x])
+    for _ in range(ways // 2):
+        earlier.append(lax.ppermute(earlier[-1], axis, up))
+    for _ in range((ways - 1) // 2):
+        later.append(lax.ppermute(later[-1], axis, down))
+    line = jnp.concatenate([*earlier[::-1], *later[1:]], axis=dim)
+    return jnp.roll(line, (lax.axis_index(axis) - ways // 2) * x.shape[dim], axis=dim)
 
 
 def combined_all(value, axis, combine):
@@ -33,7 +46,7 @@
     token_offset = lax.axis_index("tok") * local_tokens
     positions = token_offset + jnp.arange(local_tokens, dtype=jnp.int32)
     usable = positions[None, :] < (LP - pad_counts)[:, None]
-    gathered = lax.all_gather(queries, "pages", axis=0, tiled=True)
+    gathered = ring_gather(queries, "pages", 0)
     query_total = gathered.shape[0]
     row_count = query_total * query_len
     query_rows = gathered.reshape(row_count, feature_width)

time: 113 us -> 141 us (1.25)
  starting transfers between devices: 0.04 us -> 31.6 us
  blocking collectives: 38.1 us -> 13.9 us
  waiting for transfers between devices: 52.9 us -> 71.9 us
  local copies, waits for them, and re-layouts: 1.7 us -> 3.56 us
    ppermute x0 -> x15, starting transfers between devices: none -> 31.6 us  [the longest x7 31 us: ring_gather(): later.append(lax.ppermute(later[-1], axis, down))]
    all_gather x1 -> x0, blocking collectives: 24.2 us -> none  [on_device(): gathered = lax.all_gather(queries, 'pages', axis=0, tiled=True)]
    ppermute x0 -> x15, waiting for transfers between devices: none -> 15.9 us  [the longest x8 14.7 us: ring_gather(): earlier.append(lax.ppermute(earlier[-1], axis, up))]
    reduce_scatter x1, waiting for transfers between devices: 52.9 us -> 56 us  [on_device(): lax.psum_scatter(query_terms, 'pages', scatter_dimension=0, tiled=True)]
    unnamed x6 -> x39, local copies, waits for them, and re-layouts: 1.31 us -> 3.14 us
  transfers between devices with their start and end apart: 1 -> 16, of which waited for: 1 -> 14; matrix products, arithmetic and copies ran while one was open for 1% -> 1% of each run, Pallas kernels for 0% -> 0%
where the time goes in v1:
time: 141 us
  waiting for transfers between devices  71.9 us (51%)
  starting transfers between devices  31.6 us (22%)
  between operations  14.9 us (11%)
  blocking collectives  13.9 us (10%)
  local copies, waits for them, and re-layouts  3.56 us (3%)
  matrix products  2.87 us (2%)
  other arithmetic  2.05 us (1%)
    reduce_scatter x1, waiting for transfers between devices, on_device(): lax.psum_scatter(query_terms, 'pages', scatter_dimension=0, tiled=True)  56 us
    ppermute x7, starting transfers between devices, ring_gather(): later.append(lax.ppermute(later[-1], axis, down))  31 us
    ppermute x8, waiting for transfers between devices, ring_gather(): earlier.append(lax.ppermute(earlier[-1], axis, up))  14.7 us
    psum x1, blocking collectives, on_device(): owned = lax.psum(owned, 'tok')  9.57 us
    all_gather x1, blocking collectives, combined_all(): everything = lax.all_gather(value, axis)  4.36 us
    unnamed x39, local copies, waits for them, and re-layouts  3.14 us
  transfers between devices with their start and end apart: 16, of which 14 were waited for; matrix products, arithmetic and copies ran while one was open for 1% of the time, Pallas kernels for 0%

profile of v1, /device:TPU:0, one launch (start us, length us, event | category | flops | bytes accessed | tf_op | source)
XLA Modules:
  0.0 140.9 jit_solution(4774161091867445454)
XLA Ops:
  7.2 0.5 collective-permute-start
  7.8 6.6 %collective-permute-done = bf16[2,32,128]{2,1,0:T(8,128)(2,1)S(1)} collective-permute-done((bf16[2,32,128]{2,1,0:T(8,128)(2,1)}, bf16[2,32,128]{2,1,0:T(8,128)(2,1)S(1)}, u32[]{:S(2)}, u32[]{:S(2)}) %collective-permute-start) | collective-permute-done | bytes 16416 | tf_op jit(solution)/shard_map/ppermute | solution.py:20
  14.3 4.4 %collective-permute-start.8 = (bf16[2,32,128]{2,1,0:T(8,128)(2,1)}, bf16[2,32,128]{2,1,0:T(8,128)(2,1)S(1)}, u32[]{:S(2)}, u32[]{:S(2)}) collective-permute-start(bf16[2,32,128]{2,1,0:T(8,128)(2,1)} %param.8), channel_id=1, source_target_pairs={{0,30},{2,0},{4,2},{6,4},{8,6},{10,8},{12,10},{14,12},{16,14},{18,... | collective-permute-start | bytes 49160 | tf_op jit(solution)/shard_map/ppermute | solution.py:22
  18.8 1.4 %collective-permute-done.1 = bf16[2,32,128]{2,1,0:T(8,128)(2,1)S(1)} collective-permute-done((bf16[2,32,128]{2,1,0:T(8,128)(2,1)S(1)}, bf16[2,32,128]{2,1,0:T(8,128)(2,1)S(1)}, u32[]{:S(2)}, u32[]{:S(2)}) %collective-permute-start.1) | collective-permute-done | bytes 16416 | tf_op jit(solution)/shard_map/ppermute | solution.py:20
  20.4 4.4 %collective-permute-start.9 = (bf16[2,32,128]{2,1,0:T(8,128)(2,1)S(1)}, bf16[2,32,128]{2,1,0:T(8,128)(2,1)S(1)}, u32[]{:S(2)}, u32[]{:S(2)}) collective-permute-start(bf16[2,32,128]{2,1,0:T(8,128)(2,1)S(1)} %collective-permute-done.8), channel_id=1, source_target_pairs={{0,30},{2,0},{4,2},{6,4},{8,6},{10,8},{12,10},{14,12},{16,14},{18,... | collective-permute-start | bytes 49160 | tf_op jit(solution)/shard_map/ppermute | solution.py:22
  24.9 1.2 collective-permute-done.2
  26.3 4.4 %collective-permute-start.10 = (bf16[2,32,128]{2,1,0:T(8,128)(2,1)S(1)}, bf16[2,32,128]{2,1,0:T(8,128)(2,1)S(1)}, u32[]{:S(2)}, u32[]{:S(2)}) collective-permute-start(bf16[2,32,128]{2,1,0:T(8,128)(2,1)S(1)} %collective-permute-done.9), channel_id=1, source_target_pairs={{0,30},{2,0},{4,2},{6,4},{8,6},{10,8},{12,10},{14,12},{16,14},{18,... | collective-permute-start | bytes 49160 | tf_op jit(solution)/shard_map/ppermute | solution.py:22
  30.7 1.2 collective-permute-done.3
  32.2 4.4 %collective-permute-start.11 = (bf16[2,32,128]{2,1,0:T(8,128)(2,1)S(1)}, bf16[2,32,128]{2,1,0:T(8,128)(2,1)S(1)}, u32[]{:S(2)}, u32[]{:S(2)}) collective-permute-start(bf16[2,32,128]{2,1,0:T(8,128)(2,1)S(1)} %collective-permute-done.10), channel_id=1, source_target_pairs={{0,30},{2,0},{4,2},{6,4},{8,6},{10,8},{12,10},{14,12},{16,14},{18,... | collective-permute-start | bytes 49160 | tf_op jit(solution)/shard_map/ppermute | solution.py:22
  36.6 1.2 collective-permute-done.4
  38.0 4.4 %collective-permute-start.12 = (bf16[2,32,128]{2,1,0:T(8,128)(2,1)S(1)}, bf16[2,32,128]{2,1,0:T(8,128)(2,1)S(1)}, u32[]{:S(2)}, u32[]{:S(2)}) collective-permute-start(bf16[2,32,128]{2,1,0:T(8,128)(2,1)S(1)} %collective-permute-done.11), channel_id=1, source_target_pairs={{0,30},{2,0},{4,2},{6,4},{8,6},{10,8},{12,10},{14,12},{16,14},{18,... | collective-permute-start | bytes 49160 | tf_op jit(solution)/shard_map/ppermute | solution.py:22
  42.4 1.2 collective-permute-done.5
  43.9 4.4 %collective-permute-start.13 = (bf16[2,32,128]{2,1,0:T(8,128)(2,1)S(1)}, bf16[2,32,128]{2,1,0:T(8,128)(2,1)S(1)}, u32[]{:S(2)}, u32[]{:S(2)}) collective-permute-start(bf16[2,32,128]{2,1,0:T(8,128)(2,1)S(1)} %collective-permute-done.12), channel_id=1, source_target_pairs={{0,30},{2,0},{4,2},{6,4},{8,6},{10,8},{12,10},{14,12},{16,14},{18,... | collective-permute-start | bytes 49160 | tf_op jit(solution)/shard_map/ppermute | solution.py:22
  48.3 1.2 collective-permute-done.6
  50.2 4.5 %collective-permute-start.14 = (bf16[2,32,128]{2,1,0:T(8,128)(2,1)S(1)}, bf16[2,32,128]{2,1,0:T(8,128)(2,1)S(1)}, u32[]{:S(2)}, u32[]{:S(2)}) collective-permute-start(bf16[2,32,128]{2,1,0:T(8,128)(2,1)S(1)} %collective-permute-done.13), channel_id=1, source_target_pairs={{0,30},{2,0},{4,2},{6,4},{8,6},{10,8},{12,10},{14,12},{16,14},{18,... | collective-permute-start | bytes 49160 | tf_op jit(solution)/shard_map/ppermute | solution.py:22
  54.7 0.7 collective-permute-done.7
  55.5 0.7 copy-done.2
  56.5 0.8 copy-done
  57.4 1.2 while.35
  57.4 0.3 fusion.38
  58.6 4.4 %all-gather = f32[2048,1]{0,1:T(1,128)S(1)} all-gather(f32[1024,1]{0,1:T(1,128)S(1)} %get-tuple-element.249), channel_id=2, replica_groups=mesh['pages'=16,'tok'=2] {'tok'}, dimensions={0}, use_global_device_ids=true | all-gather | bytes 12288 | tf_op jit(solution)/shard_map/all_gather | solution.py:28
  63.2 0.5 copy-done.3
  63.8 0.6 fusion.24
  64.6 2.4 %while.36 = (s32[]{:T(128)}, f32[1024,128]{1,0:T(8,128)S(1)}, f32[1,512,128]{2,1,0:T(8,128)S(1)}, bf16[1024,128]{1,0:T(8,128)(2,1)S(1)}, bf16[1,512,128]{2,1,0:T...) while((s32[]{:T(128)}, f32[1024,128]{1,0:T(8,128)S(1)}, ...), condition=%wide.region_6.7_spmd.clone, body=%wide.region_5.6_spmd.clone.sunk | while | flops 203097088 | bytes 2897109 | solution.py:113
  64.7 0.4 fusion.45
  65.1 0.4 fusion.47
  65.9 0.4 fusion.45
  66.3 0.4 fusion.47
  67.0 0.8 copy-done.1
  67.8 0.7 broadcast_multiply_fusion
  68.5 56.0 %reduce-scatter.2.cloned.1.call-done = f32[64,128]{1,0:T(8,128)} async-done(((f32[1024,128]{1,0:T(8,128)}), f32[64,128]{1,0:T(8,128)}) %reduce-scatter.2.cloned.1.call-update) | async-done | bytes 32784 | tf_op jit(solution)/shard_map/reduce_scatter | solution.py:115
  124.5 9.6 %psum.7 = f32[2,32,128]{2,1,0:T(8,128)} all-reduce(f32[2,32,128]{2,1,0:T(8,128)} %bitcast.50), channel_id=1, replica_groups=mesh['pages'=16,'tok'=2] {'tok'}, use_global_device_ids=true, to_apply=%region_8.9 | all-reduce | flops 8192 | bytes 65536 | tf_op jit(solution)/shard_map/psum | solution.py:116
  (78 shorter events, 3.6 us)
Async XLA Ops:
  7.2 117.4 %reduce-scatter.2.cloned.1.call-start = ((), (), s32[]{:S(2)}) async-start(), calls=%async_computation.1 | async-start | bytes 557056 | tf_op jit(solution)/shard_map/reduce_scatter | solution.py:115
  7.2 7.1 %collective-permute-start = (bf16[2,32,128]{2,1,0:T(8,128)(2,1)}, bf16[2,32,128]{2,1,0:T(8,128)(2,1)S(1)}, u32[]{:S(2)}, u32[]{:S(2)}) collective-permute-start(bf16[2,32,128]{2,1,0:T(8,128)(2,1)} %param.8), channel_id=1, source_target_pairs={{0,2},{2,4},{4,6},{6,8},{8,10},{10,12},{12,14},{14,16},{16,18},{18... | collective-permute-start | bytes 49160 | tf_op jit(solution)/shard_map/ppermute | solution.py:20
  14.3 5.9 %collective-permute-start.1 = (bf16[2,32,128]{2,1,0:T(8,128)(2,1)S(1)}, bf16[2,32,128]{2,1,0:T(8,128)(2,1)S(1)}, u32[]{:S(2)}, u32[]{:S(2)}) collective-permute-start(bf16[2,32,128]{2,1,0:T(8,128)(2,1)S(1)} %collective-permute-done), channel_id=1, source_target_pairs={{0,2},{2,4},{4,6},{6,8},{8,10},{10,12},{12,14},{14,16},{16,18},{18... | collective-permute-start | bytes 49160 | tf_op jit(solution)/shard_map/ppermute | solution.py:20
  14.3 6.1 %collective-permute-start.8 = (bf16[2,32,128]{2,1,0:T(8,128)(2,1)}, bf16[2,32,128]{2,1,0:T(8,128)(2,1)S(1)}, u32[]{:S(2)}, u32[]{:S(2)}) collective-permute-start(bf16[2,32,128]{2,1,0:T(8,128)(2,1)} %param.8), channel_id=1, source_target_pairs={{0,30},{2,0},{4,2},{6,4},{8,6},{10,8},{12,10},{14,12},{16,14},{18,... | collective-permute-start | bytes 49160 | tf_op jit(solution)/shard_map/ppermute | solution.py:22
  20.2 5.9 %collective-permute-start.2 = (bf16[2,32,128]{2,1,0:T(8,128)(2,1)S(1)}, bf16[2,32,128]{2,1,0:T(8,128)(2,1)S(1)}, u32[]{:S(2)}, u32[]{:S(2)}) collective-permute-start(bf16[2,32,128]{2,1,0:T(8,128)(2,1)S(1)} %collective-permute-done.1), channel_id=1, source_target_pairs={{0,2},{2,4},{4,6},{6,8},{8,10},{10,12},{12,14},{14,16},{16,18},{18... | collective-permute-start | bytes 49160 | tf_op jit(solution)/shard_map/ppermute | solution.py:20
  20.4 5.9 %collective-permute-start.9 = (bf16[2,32,128]{2,1,0:T(8,128)(2,1)S(1)}, bf16[2,32,128]{2,1,0:T(8,128)(2,1)S(1)}, u32[]{:S(2)}, u32[]{:S(2)}) collective-permute-start(bf16[2,32,128]{2,1,0:T(8,128)(2,1)S(1)} %collective-permute-done.8), channel_id=1, source_target_pairs={{0,30},{2,0},{4,2},{6,4},{8,6},{10,8},{12,10},{14,12},{16,14},{18,... | collective-permute-start | bytes 49160 | tf_op jit(solution)/shard_map/ppermute | solution.py:22
  26.1 5.9 %collective-permute-start.3 = (bf16[2,32,128]{2,1,0:T(8,128)(2,1)S(1)}, bf16[2,32,128]{2,1,0:T(8,128)(2,1)S(1)}, u32[]{:S(2)}, u32[]{:S(2)}) collective-permute-start(bf16[2,32,128]{2,1,0:T(8,128)(2,1)S(1)} %collective-permute-done.2), channel_id=1, source_target_pairs={{0,2},{2,4},{4,6},{6,8},{8,10},{10,12},{12,14},{14,16},{16,18},{18... | collective-permute-start | bytes 49160 | tf_op jit(solution)/shard_map/ppermute | solution.py:20
  26.3 5.9 %collective-permute-start.10 = (bf16[2,32,128]{2,1,0:T(8,128)(2,1)S(1)}, bf16[2,32,128]{2,1,0:T(8,128)(2,1)S(1)}, u32[]{:S(2)}, u32[]{:S(2)}) collective-permute-start(bf16[2,32,128]{2,1,0:T(8,128)(2,1)S(1)} %collective-permute-done.9), channel_id=1, source_target_pairs={{0,30},{2,0},{4,2},{6,4},{8,6},{10,8},{12,10},{14,12},{16,14},{18,... | collective-permute-start | bytes 49160 | tf_op jit(solution)/shard_map/ppermute | solution.py:22
  31.9 5.9 %collective-permute-start.4 = (bf16[2,32,128]{2,1,0:T(8,128)(2,1)S(1)}, bf16[2,32,128]{2,1,0:T(8,128)(2,1)S(1)}, u32[]{:S(2)}, u32[]{:S(2)}) collective-permute-start(bf16[2,32,128]{2,1,0:T(8,128)(2,1)S(1)} %collective-permute-done.3), channel_id=1, source_target_pairs={{0,2},{2,4},{4,6},{6,8},{8,10},{10,12},{12,14},{14,16},{16,18},{18... | collective-permute-start | bytes 49160 | tf_op jit(solution)/shard_map/ppermute | solution.py:20
  32.2 5.9 %collective-permute-start.11 = (bf16[2,32,128]{2,1,0:T(8,128)(2,1)S(1)}, bf16[2,32,128]{2,1,0:T(8,128)(2,1)S(1)}, u32[]{:S(2)}, u32[]{:S(2)}) collective-permute-start(bf16[2,32,128]{2,1,0:T(8,128)(2,1)S(1)} %collective-permute-done.10), channel_id=1, source_target_pairs={{0,30},{2,0},{4,2},{6,4},{8,6},{10,8},{12,10},{14,12},{16,14},{18,... | collective-permute-start | bytes 49160 | tf_op jit(solution)/shard_map/ppermute | solution.py:22
  37.8 5.9 %collective-permute-start.5 = (bf16[2,32,128]{2,1,0:T(8,128)(2,1)S(1)}, bf16[2,32,128]{2,1,0:T(8,128)(2,1)S(1)}, u32[]{:S(2)}, u32[]{:S(2)}) collective-permute-start(bf16[2,32,128]{2,1,0:T(8,128)(2,1)S(1)} %collective-permute-done.4), channel_id=1, source_target_pairs={{0,2},{2,4},{4,6},{6,8},{8,10},{10,12},{12,14},{14,16},{16,18},{18... | collective-permute-start | bytes 49160 | tf_op jit(solution)/shard_map/ppermute | solution.py:20
  38.0 5.9 %collective-permute-start.12 = (bf16[2,32,128]{2,1,0:T(8,128)(2,1)S(1)}, bf16[2,32,128]{2,1,0:T(8,128)(2,1)S(1)}, u32[]{:S(2)}, u32[]{:S(2)}) collective-permute-start(bf16[2,32,128]{2,1,0:T(8,128)(2,1)S(1)} %collective-permute-done.11), channel_id=1, source_target_pairs={{0,30},{2,0},{4,2},{6,4},{8,6},{10,8},{12,10},{14,12},{16,14},{18,... | collective-permute-start | bytes 49160 | tf_op jit(solution)/shard_map/ppermute | solution.py:22
  43.7 5.9 %collective-permute-start.6 = (bf16[2,32,128]{2,1,0:T(8,128)(2,1)S(1)}, bf16[2,32,128]{2,1,0:T(8,128)(2,1)S(1)}, u32[]{:S(2)}, u32[]{:S(2)}) collective-permute-start(bf16[2,32,128]{2,1,0:T(8,128)(2,1)S(1)} %collective-permute-done.5), channel_id=1, source_target_pairs={{0,2},{2,4},{4,6},{6,8},{8,10},{10,12},{12,14},{14,16},{16,18},{18... | collective-permute-start | bytes 49160 | tf_op jit(solution)/shard_map/ppermute | solution.py:20
  43.9 6.3 %collective-permute-start.13 = (bf16[2,32,128]{2,1,0:T(8,128)(2,1)S(1)}, bf16[2,32,128]{2,1,0:T(8,128)(2,1)S(1)}, u32[]{:S(2)}, u32[]{:S(2)}) collective-permute-start(bf16[2,32,128]{2,1,0:T(8,128)(2,1)S(1)} %collective-permute-done.12), channel_id=1, source_target_pairs={{0,30},{2,0},{4,2},{6,4},{8,6},{10,8},{12,10},{14,12},{16,14},{18,... | collective-permute-start | bytes 49160 | tf_op jit(solution)/shard_map/ppermute | solution.py:22
  49.5 5.9 %collective-permute-start.7 = (bf16[2,32,128]{2,1,0:T(8,128)(2,1)S(1)}, bf16[2,32,128]{2,1,0:T(8,128)(2,1)S(1)}, u32[]{:S(2)}, u32[]{:S(2)}) collective-permute-start(bf16[2,32,128]{2,1,0:T(8,128)(2,1)S(1)} %collective-permute-done.6), channel_id=1, source_target_pairs={{0,2},{2,4},{4,6},{6,8},{8,10},{10,12},{12,14},{14,16},{16,18},{18... | collective-permute-start | bytes 49160 | tf_op jit(solution)/shard_map/ppermute | solution.py:20
  50.2 6.1 %collective-permute-start.14 = (bf16[2,32,128]{2,1,0:T(8,128)(2,1)S(1)}, bf16[2,32,128]{2,1,0:T(8,128)(2,1)S(1)}, u32[]{:S(2)}, u32[]{:S(2)}) collective-permute-start(bf16[2,32,128]{2,1,0:T(8,128)(2,1)S(1)} %collective-permute-done.13), channel_id=1, source_target_pairs={{0,30},{2,0},{4,2},{6,4},{8,6},{10,8},{12,10},{14,12},{16,14},{18,... | collective-permute-start | bytes 49160 | tf_op jit(solution)/shard_map/ppermute | solution.py:22
  55.4 0.7 copy-start.2
  56.5 0.9 copy-start
  63.1 0.7 copy-start.3
  67.0 0.8 copy-start.1
Sparse Core Ops, SparseCore 0:
  67.9 56.5 reduce-scatter.1
